TPU v7x, 32 devices: a whole 2x2x4 slice. The times are simulated.
32 devices in a mesh: groups: 2 (over y), snap: 4 (over x, core), space: 4 (over z).
Axes of the slice: x: 2, y: 2, z: 4, core: 2. Of those that a mesh axis runs over, the one named last changes fastest.
Arguments:
- snapshots: bfloat16 [16384, 4096], P('space', ('groups', 'snap')), parts along dimension 1, may hold values from -12 to 12
- factor_blocks: bfloat16 [128, 4, 128, 128], P('space'), may hold values from -0.375 to 0.375
- factor_cols: int32 [128, 4], P('space'), may hold values from 0 to 31, as said below
- factor_counts: int32 [128], P('space'), may hold values from 1 to 4, as said below
- start_basis: float32 [4096, 128], P(('groups', 'snap')), parts along dimension 0, may hold values from -150 to 150
- merge_starts: float32 [3, 256, 128], replicated, may hold values from -150 to 150
Outputs:
- modes: bfloat16 [16384, 256], P(('space', 'snap'), 'groups'), parts along dimension 1
There are 2 independent parts, one for each index of `groups`. A program takes and returns all parts, laid end to end along the dimension named above; an argument that names none is the same for every part. Nothing has to cross between parts.
Inputs may be any that keep to these rules, and one draw needn't show every extreme that they name: `factor_cols`: each entry names one of the 32 row blocks of the same group as its row block. `factor_counts`: slots at or after the count are not part of the factor.
All inputs are finite; a program needn't handle non-finite values.
Results may differ from a plain program's by a relative error of at most 0.011.
Values may be sent and summed in bfloat16 or wider, within the bound.
A program may use at most 128 MiB of HBM per device.

v0:
```python
import jax
import jax.numpy as jnp
from jax import lax
from jax.sharding import PartitionSpec as P

HIGH = lax.Precision.HIGHEST


def from_partner(block, axis, bit):
    count = lax.axis_size(axis)
    route = []
    for low in range(count):
        high = low | 1 << bit
        if high != low and high < count:
            route += [(low, high), (high, low)]
    return lax.ppermute(block, axis, route)


def orthonormal(matrix):
    cross_gram = jnp.dot(matrix.T, matrix, precision=HIGH)
    lower_factor = jnp.linalg.cholesky(cross_gram)
    return lax.linalg.triangular_solve(
        lower_factor, matrix, left_side=False, lower=True, transpose_a=True
    )


def weigh(snapshots, factor_blocks, factor_cols, factor_counts):
    row_blocks, slot_count = factor_cols.shape
    block_width = factor_blocks.shape[2]
    column_count = snapshots.shape[1]
    blocks_in = snapshots.reshape(row_blocks, block_width, column_count)
    accumulated = jnp.zeros((row_blocks, block_width, column_count), jnp.float32)
    for slot_index in range(slot_count):
        live_mask = (slot_index < factor_counts)[:, None, None]
        factor = jnp.where(live_mask, factor_blocks[:, slot_index], jnp.zeros((), jnp.bfloat16))
        source = jnp.take(blocks_in, factor_cols[:, slot_index], axis=0)
        accumulated = accumulated + jnp.einsum(
            "bij,bjs->bis", factor, source, preferred_element_type=jnp.float32
        )
    return accumulated.astype(jnp.bfloat16).reshape(row_blocks * block_width, column_count)


def merge_level(paired, start_vectors, summed):
    local_cross = jnp.einsum("prk,prl->pkl", paired, paired, preferred_element_type=jnp.float32)
    cross_gram = summed(local_cross)
    steered = jnp.einsum("pkl,plm->pkm", cross_gram, start_vectors, precision=HIGH)
    mixing = jax.vmap(orthonormal)(steered).astype(jnp.bfloat16)
    return jnp.einsum("prk,pkm->prm", paired, mixing, preferred_element_type=jnp.float32).astype(
        jnp.bfloat16
    )


def local(snapshots, factor_blocks, factor_cols, factor_counts, start_basis, merge_starts):
    weighted = weigh(snapshots, factor_blocks, factor_cols, factor_counts)
    basis = start_basis
    own_gram = lax.psum_scatter(
        lax.dot_general(
            weighted, weighted, (((0,), (0,)), ((), ())), preferred_element_type=jnp.float32
        ),
        "space",
        scatter_dimension=0,
        tiled=True,
    )
    for sweep_index in range(2):
        own_rows = jnp.dot(own_gram, basis, precision=HIGH)
        cross_gram = lax.psum(jnp.dot(own_rows.T, own_rows, precision=HIGH), "space")
        lower_factor = jnp.linalg.cholesky(cross_gram)
        own_basis = lax.linalg.triangular_solve(
            lower_factor, own_rows, left_side=False, lower=True, transpose_a=True
        )
        basis = lax.all_gather(own_basis, "space", axis=0, tiled=True)
    panel = jnp.dot(
        weighted, basis.astype(jnp.bfloat16), preferred_element_type=jnp.float32
    ).astype(jnp.bfloat16)
    row_count = panel.shape[0]
    snap_count = lax.axis_size("snap")
    levels = snap_count.bit_length() - 1
    snap_index = lax.axis_index("snap")
    for level_index in range(levels):
        partner = from_partner(panel, "snap", level_index)
        upper_side = snap_index >> level_index & 1 == 1
        paired = jnp.where(
            upper_side,
            jnp.concatenate([partner, panel], axis=1),
            jnp.concatenate([panel, partner], axis=1),
        )
        merge_index = snap_count - (snap_count >> level_index) + (snap_index >> level_index + 1)
        start_vectors = lax.dynamic_index_in_dim(merge_starts, merge_index, 0, keepdims=True)
        panel = merge_level(paired[None], start_vectors, lambda grams: lax.psum(grams, "space"))[0]
    own_count = row_count // snap_count
    return lax.dynamic_slice_in_dim(panel, lax.axis_index("snap") * own_count, own_count, 0)


def solution(mesh):
    return jax.shard_map(
        local,
        mesh=mesh,
        in_specs=(
            P("space", ("groups", "snap")),
            P("space", None, None, None),
            P("space", None),
            P("space"),
            P(("groups", "snap"), None),
            P(),
        ),
        out_specs=P(("space", "snap"), "groups"),
        check_vma=False,
    )
```

profile of v0, /device:TPU:0, one launch (start us, length us, event | category | flops | bytes accessed | tf_op | source)
XLA Modules:
  0.0 403.9 jit_solution(3854561859859952398)
XLA Ops:
  7.4 5.0 %gather_fusion.2 = bf16[32,128,512]{2,1,0:T(8,128)(2,1)} fusion(bf16[32,128,512]{2,1,0:T(8,128)(2,1)} %bitcast.131, s32[1024]{0:T(1024)S(1)} %pad_clamp_fusion.1), kind=kCustom, calls=%fused_computation.2.clone | custom fusion | bytes 8388736 | tf_op jit(solution)/shard_map/jit(_take)/gather | solution.py:36
  12.4 5.0 %gather_fusion.1 = bf16[32,128,512]{2,1,0:T(8,128)(2,1)} fusion(bf16[32,128,512]{2,1,0:T(8,128)(2,1)} %bitcast.132, s32[1024]{0:T(1024)S(1)} %pad_clamp_fusion.2), kind=kCustom, calls=%fused_computation.1.clone | custom fusion | bytes 8388736 | tf_op jit(solution)/shard_map/jit(_take)/gather | solution.py:36
  17.4 4.9 %gather_fusion.3 = bf16[32,128,512]{2,1,0:T(8,128)(2,1)} fusion(bf16[32,128,512]{2,1,0:T(8,128)(2,1)} %bitcast.133, s32[1024]{0:T(1024)S(1)} %pad_clamp_fusion), kind=kCustom, calls=%fused_computation.3.clone | custom fusion | bytes 8388736 | tf_op jit(solution)/shard_map/jit(_take)/gather | solution.py:36
  22.3 5.0 %gather_fusion = bf16[32,128,512]{2,1,0:T(8,128)(2,1)} fusion(bf16[32,128,512]{2,1,0:T(8,128)(2,1)} %bitcast.134, s32[1024]{0:T(1024)S(1)} %pad_clamp_fusion.3), kind=kCustom, calls=%fused_computation.clone | custom fusion | bytes 8388736 | tf_op jit(solution)/shard_map/jit(_take)/gather | solution.py:36
  27.3 7.2 %fusion.2 = f32[32,128,512]{2,1,0:T(8,128)} fusion(bf16[32,128,512]{2,1,0:T(8,128)(2,1)} %gather_fusion.2, pred[32]{0:T(512)(128)(4,1)S(1)} %get-tuple-element.22, bf16[32,4,128,128]{3,2,1,0:T(8,128)(2,1)} %param.15, pred[32]{0:T(512)(128)(4,1)S(1)} %get-tuple-element.28), kind=kOutput, calls=%fused_computation.9 | convolution fusion | flops 539492352 | bytes 13631552 | tf_op jit(solution)/shard_map/bij,bjs->bis/dot_general | solution.py:37
  34.5 4.5 %fusion.4 = f32[32,128,512]{2,1,0:T(8,128)} fusion(bf16[32,128,512]{2,1,0:T(8,128)(2,1)S(1)} %copy-done.2, pred[32]{0:T(512)(128)(4,1)S(1)} %get-tuple-element.18, bf16[32,4,128,128]{3,2,1,0:T(8,128)(2,1)S(1)} %copy-done.4, pred[32]{0:T(512)(128)(4,1)S(1)} %get-tuple-element.30), kind=kOutput, calls=%fused_computation.11 | convolution fusion | flops 539492352 | bytes 13632512 | tf_op jit(solution)/shard_map/bij,bjs->bis/dot_general | solution.py:37
  39.0 4.5 %fusion = f32[32,128,512]{2,1,0:T(8,128)} fusion(bf16[32,128,512]{2,1,0:T(8,128)(2,1)S(1)} %copy-done.3, pred[32]{0:T(512)(128)(4,1)S(1)} %get-tuple-element.20, bf16[32,4,128,128]{3,2,1,0:T(8,128)(2,1)S(1)} %copy-done.4, pred[32]{0:T(512)(128)(4,1)S(1)} %get-tuple-element.29), kind=kOutput, calls=%fused_computation.7 | convolution fusion | flops 539492352 | bytes 13632512 | tf_op jit(solution)/shard_map/bij,bjs->bis/dot_general | solution.py:37
  43.5 11.6 %add_convert_fusion = bf16[32,128,512]{2,1,0:T(8,128)(2,1)S(1)} fusion(f32[32,128,512]{2,1,0:T(8,128)} %fusion, f32[32,128,512]{2,1,0:T(8,128)} %fusion.2, f32[32,128,512]{2,1,0:T(8,128)} %fusion.4, bf16[32,128,512]{2,1,0:T(8,128)(2,1)} %gather_fusion, pred[32]{0:T(512)(128)(4,1)S(1)} %get-tuple-element.6, bf16[32,4,128,128]{3,2,1,0:T(8,128)(2,1)} %param.15, ...), kind=kOutput, calls=%fused_computation.4 | convolution fusion | flops 547880960 | bytes 34603072 | tf_op jit(solution)/shard_map/bij,bjs->bis/dot_general | solution.py:37
  60.5 30.1 %reduce-scatter.2.cloned.1.call-done = f32[128,512]{1,0:T(8,128)} async-done(((f32[512,512]{1,0:T(8,128)}), f32[128,512]{1,0:T(8,128)}) %reduce-scatter.2.cloned.1.call-update) | async-done | bytes 262160 | tf_op jit(solution)/shard_map/reduce_scatter | solution.py:56
  93.5 32.4 %all-reduce.5.cloned.1.call-done = f32[128,128]{0,1:T(8,128)} async-done(((f32[128,128]{0,1:T(8,128)}), f32[128,128]{0,1:T(8,128)}) %all-reduce.5.cloned.1.call-update) | async-done | bytes 65552 | tf_op jit(solution)/shard_map/psum | solution.py:66
  127.7 11.7 %cholesky.84 = f32[128,128]{1,0:T(8,128)S(1)} custom-call(f32[128,128]{1,0:T(8,128)S(1)} %fusion.55), custom_call_target="Cholesky" | custom-call | tf_op jit(solution)/shard_map/jit(cholesky)/cholesky | solution.py:67
  140.7 9.8 %custom-call.14 = f32[1,128,128]{1,2,0:T(8,128)S(1)} custom-call(f32[1,128,128]{2,1,0:T(8,128)S(1)} %fusion.44), custom_call_target="InvertDiagBlocksLowerTriangular" | custom-call | tf_op jit(solution)/shard_map/triangular_solve/custom-call.2 | solution.py:68
  150.8 14.4 %all_gather.6 = f32[512,128]{0,1:T(8,128)S(1)} all-gather(f32[128,128]{0,1:T(8,128)S(1)} %convolution_bitcast_fusion.4), channel_id=1, replica_groups=mesh['groups'=2,'snap'=4,'space'=4] {'space'}, dimensions={0}, use_global_device_ids=true | all-gather | bytes 327680 | tf_op jit(solution)/shard_map/all_gather | solution.py:71
  167.7 33.4 %all-reduce.7.cloned.1.call-done = f32[128,128]{0,1:T(8,128)} async-done(((f32[128,128]{0,1:T(8,128)}), f32[128,128]{0,1:T(8,128)}) %all-reduce.7.cloned.1.call-update) | async-done | bytes 65552 | tf_op jit(solution)/shard_map/psum | solution.py:66
  202.9 11.7 %cholesky.95 = f32[128,128]{1,0:T(8,128)S(1)} custom-call(f32[128,128]{1,0:T(8,128)S(1)} %fusion.53), custom_call_target="Cholesky" | custom-call | tf_op jit(solution)/shard_map/jit(cholesky)/cholesky | solution.py:67
  216.0 9.8 %custom-call.15 = f32[1,128,128]{1,2,0:T(8,128)S(1)} custom-call(f32[1,128,128]{2,1,0:T(8,128)S(1)} %fusion.45), custom_call_target="InvertDiagBlocksLowerTriangular" | custom-call | tf_op jit(solution)/shard_map/triangular_solve/custom-call.2 | solution.py:68
  226.1 12.3 %all_gather.7 = bf16[512,128]{0,1:T(8,128)(2,1)S(1)} all-gather(bf16[128,128]{0,1:T(8,128)(2,1)S(1)} %convolution_bitcast_fusion.3), channel_id=1, replica_groups=mesh['groups'=2,'snap'=4,'space'=4] {'space'}, dimensions={0}, use_global_device_ids=true | all-gather | bytes 163840 | tf_op jit(solution)/shard_map/all_gather | solution.py:71
  246.8 34.0 %all-reduce.9.cloned.1.call-done = f32[256,256]{1,0:T(8,128)} async-done(((f32[256,256]{1,0:T(8,128)}), f32[256,256]{1,0:T(8,128)}) %all-reduce.9.cloned.1.call-update) | async-done | bytes 262160 | tf_op jit(solution)/shard_map/psum | solution.py:89
  282.7 11.7 %custom-call.16 = f32[1,128,128]{2,1,0:T(8,128)S(1)} custom-call(f32[1,128,128]{2,1,0:T(8,128)S(1)} %fusion.49), custom_call_target="Cholesky" | custom-call | tf_op jit(solution)/shard_map/vmap(jit(cholesky))/cholesky | solution.py:21
  295.7 9.8 %custom-call.17 = f32[1,1,128,128]{2,3,1,0:T(8,128)S(1)} custom-call(f32[1,1,128,128]{3,2,1,0:T(8,128)S(1)} %fusion.46), custom_call_target="InvertDiagBlocksLowerTriangular" | custom-call | tf_op jit(solution)/shard_map/vmap()/triangular_solve/custom-call.3 | solution.py:22
  309.8 21.3 %collective-permute-done.1 = bf16[4096,128]{0,1:T(8,128)(2,1)S(1)} collective-permute-done((bf16[4096,128]{0,1:T(8,128)(2,1)S(1)}, bf16[4096,128]{0,1:T(8,128)(2,1)S(1)}, u32[]{:S(2)}, u32[]{:S(2)}) %collective-permute-start.1) | collective-permute-done | bytes 1048608 | tf_op jit(solution)/shard_map/ppermute | solution.py:16
  333.0 35.6 %all-reduce.11.cloned.1.call-done = f32[256,256]{1,0:T(8,128)} async-done(((f32[256,256]{1,0:T(8,128)}), f32[256,256]{1,0:T(8,128)}) %all-reduce.11.cloned.1.call-update) | async-done | bytes 262160 | tf_op jit(solution)/shard_map/psum | solution.py:89
  370.4 11.9 %custom-call.18 = f32[1,128,128]{2,1,0:T(8,128)S(1)} custom-call(f32[1,128,128]{2,1,0:T(8,128)S(1)} %fusion.48), custom_call_target="Cholesky" | custom-call | tf_op jit(solution)/shard_map/vmap(jit(cholesky))/cholesky | solution.py:21
  383.7 9.8 %custom-call.19 = f32[1,1,128,128]{2,3,1,0:T(8,128)S(1)} custom-call(f32[1,1,128,128]{3,2,1,0:T(8,128)S(1)} %fusion.47), custom_call_target="InvertDiagBlocksLowerTriangular" | custom-call | tf_op jit(solution)/shard_map/vmap()/triangular_solve/custom-call.3 | solution.py:22
  (73 shorter events, 42.6 us)
Async XLA Ops:
  6.5 274.3 %copy-start = (f32[3,256,128]{2,1,0:T(8,128)S(1)}, f32[3,256,128]{2,1,0:T(8,128)}, u32[]{:S(2)}) copy-start(f32[3,256,128]{2,1,0:T(8,128)} %param.19) | copy-start | bytes 1179652
  6.5 84.1 %reduce-scatter.2.cloned.1.call-start = ((), (), s32[]{:S(2)}) async-start(), calls=%async_computation.1 | async-start | bytes 1310720 | tf_op jit(solution)/shard_map/reduce_scatter | solution.py:56
  27.3 7.2 %copy-start.2 = (bf16[32,128,512]{2,1,0:T(8,128)(2,1)S(1)}, bf16[32,128,512]{2,1,0:T(8,128)(2,1)}, u32[]{:S(2)}) copy-start(bf16[32,128,512]{2,1,0:T(8,128)(2,1)} %gather_fusion.1) | copy-start | bytes 12582916
  27.3 7.2 %copy-start.4 = (bf16[32,4,128,128]{3,2,1,0:T(8,128)(2,1)S(1)}, bf16[32,4,128,128]{3,2,1,0:T(8,128)(2,1)}, u32[]{:S(2)}) copy-start(bf16[32,4,128,128]{3,2,1,0:T(8,128)(2,1)} %param.15) | copy-start | bytes 12582916
  34.5 4.5 %copy-start.3 = (bf16[32,128,512]{2,1,0:T(8,128)(2,1)S(1)}, bf16[32,128,512]{2,1,0:T(8,128)(2,1)}, u32[]{:S(2)}) copy-start(bf16[32,128,512]{2,1,0:T(8,128)(2,1)} %gather_fusion.3) | copy-start | bytes 12582916
  55.2 1.9 copy-start.1
  57.1 33.5 %copy-start.5 = (f32[512,128]{1,0:T(8,128)S(1)}, f32[512,128]{1,0:T(8,128)}, u32[]{:S(2)}) copy-start(f32[512,128]{1,0:T(8,128)} %param.18) | copy-start | bytes 786436
  60.4 65.4 %all-reduce.5.cloned.1.call-start = ((), (), s32[]{:S(2)}) async-start(), calls=%async_computation.2 | async-start | bytes 131072 | tf_op jit(solution)/shard_map/psum | solution.py:66
  92.9 108.2 %all-reduce.7.cloned.1.call-start = ((), (), s32[]{:S(2)}) async-start(), calls=%async_computation.3 | async-start | bytes 131072 | tf_op jit(solution)/shard_map/psum | solution.py:66
  167.5 113.4 %all-reduce.9.cloned.1.call-start = ((), (), s32[]{:S(2)}) async-start(), calls=%async_computation.4 | async-start | bytes 524288 | tf_op jit(solution)/shard_map/psum | solution.py:89
  242.0 2.7 collective-permute-start
  244.7 1.8 copy-start.7
  246.6 122.0 %all-reduce.11.cloned.1.call-start = ((), (), s32[]{:S(2)}) async-start(), calls=%async_computation.5 | async-start | bytes 524288 | tf_op jit(solution)/shard_map/psum | solution.py:89
  308.2 22.9 %collective-permute-start.1 = (bf16[4096,128]{0,1:T(8,128)(2,1)S(1)}, bf16[4096,128]{0,1:T(8,128)(2,1)S(1)}, u32[]{:S(2)}, u32[]{:S(2)}) collective-permute-start(bf16[4096,128]{0,1:T(8,128)(2,1)S(1)} %convolution_convert_fusion), channel_id=1, source_target_pairs={{0,8},{8,0},{4,12},{12,4},{1,9},{9,1},{5,13},{13,5},{2,10},{10,2},... | collective-permute-start | bytes 3145736 | tf_op jit(solution)/shard_map/ppermute | solution.py:16
  331.1 1.8 copy-start.6
Sparse Core Ops, SparseCore 0:
  60.6 29.9 reduce-scatter.1
  93.0 32.8 all-reduce.4
  167.6 33.4 all-reduce.6
  246.7 34.0 all-reduce.8
  333.1 35.4 all-reduce.10
where the time goes:
time: 411 us; the launch traced here: 404 us
  waiting for transfers between devices  190 us (46%)
  other arithmetic  94.2 us (23%)
  matrix products  52.4 us (13%)
  blocking collectives  26.7 us (6%)
  local copies, waits for them, and re-layouts  24.6 us (6%)
  between operations  13.7 us (3%)
    psum x2, waiting for transfers between devices, local(): lax.psum(grams, 'space')  69.6 us
    psum x2, waiting for transfers between devices, local(): lax.psum(jnp.dot(own_rows.T, own_rows, precision=HIGH), 'space')  65.8 us
    reduce_scatter x1, waiting for transfers between devices, local(): lax.psum_scatter(lax.dot_general(weighted, weighted, (((0,), (0,)), ((),...  30.1 us
    dot_general x4, matrix products, weigh(): jnp.einsum('bij,bjs->bis', factor, source, preferred_element_type=jnp.flo...  27.9 us
    all_gather x2, blocking collectives, local(): basis = lax.all_gather(own_basis, 'space', axis=0, tiled=True)  26.7 us
    another operation x6, other arithmetic, orthonormal(): lower_factor = jnp.linalg.cholesky(cross_gram)  25 us
    another operation x6, other arithmetic, local(): lower_factor = jnp.linalg.cholesky(cross_gram)  24.8 us
    ppermute x2, waiting for transfers between devices, from_partner(): return lax.ppermute(block, axis, route)  24 us
  transfers between devices with their start and end apart: 7, of which 7 were waited for; matrix products, arithmetic and copies ran while one was open for 0% of the time, Pallas kernels for 0%

commit v1 on v0

--- a/solution.py
+++ b/solution.py
@@ -86,7 +86,11 @@
         )
         merge_index = snap_count - (snap_count >> level_index) + (snap_index >> level_index + 1)
         start_vectors = lax.dynamic_index_in_dim(merge_starts, merge_index, 0, keepdims=True)
-        panel = merge_level(paired[None], start_vectors, lambda grams: lax.psum(grams, "space"))[0]
+        panel = merge_level(
+            paired[None],
+            start_vectors,
+            lambda grams: jnp.sum(lax.all_gather(grams, "space"), axis=0),
+        )[0]
     own_count = row_count // snap_count
     return lax.dynamic_slice_in_dim(panel, lax.axis_index("snap") * own_count, own_count, 0)
 

time: 411 us -> 398 us (0.968)
  waiting for transfers between devices: 190 us -> 176 us
    psum x2 -> x0, waiting for transfers between devices: 69.6 us -> none  [local(): lax.psum(grams, 'space')]
    all_gather x0 -> x2, waiting for transfers between devices: none -> 54.4 us  [local(): lax.all_gather(grams, 'space')]
where the time goes in v1:
time: 398 us; the launch traced here: 391 us
  waiting for transfers between devices  176 us (44%)
  other arithmetic  96.9 us (24%)
  matrix products  50.5 us (13%)
  blocking collectives  26.7 us (7%)
  local copies, waits for them, and re-layouts  24.6 us (6%)
  between operations  13.7 us (3%)
    psum x2, waiting for transfers between devices, local(): lax.psum(jnp.dot(own_rows.T, own_rows, precision=HIGH), 'space')  65.8 us
    all_gather x2, waiting for transfers between devices, local(): lax.all_gather(grams, 'space')  54.4 us
    reduce_scatter x1, waiting for transfers between devices, local(): lax.psum_scatter(lax.dot_general(weighted, weighted, (((0,), (0,)), ((),...  30.1 us
    dot_general x4, matrix products, weigh(): jnp.einsum('bij,bjs->bis', factor, source, preferred_element_type=jnp.flo...  27.9 us
    all_gather x2, blocking collectives, local(): basis = lax.all_gather(own_basis, 'space', axis=0, tiled=True)  26.7 us
    ppermute x2, waiting for transfers between devices, from_partner(): return lax.ppermute(block, axis, route)  25.6 us
    another operation x6, other arithmetic, orthonormal(): lower_factor = jnp.linalg.cholesky(cross_gram)  25 us
    another operation x6, other arithmetic, local(): lower_factor = jnp.linalg.cholesky(cross_gram)  24.8 us
  transfers between devices with their start and end apart: 7, of which 7 were waited for; matrix products, arithmetic and copies ran while one was open for 0% of the time, Pallas kernels for 0%

profile of v1, /device:TPU:0, one launch (start us, length us, event | category | flops | bytes accessed | tf_op | source)
XLA Modules:
  0.0 391.0 jit_solution(15514256228268400841)
XLA Ops:
  7.4 5.0 %gather_fusion.2 = bf16[32,128,512]{2,1,0:T(8,128)(2,1)} fusion(bf16[32,128,512]{2,1,0:T(8,128)(2,1)} %bitcast.133, s32[1024]{0:T(1024)S(1)} %pad_clamp_fusion.1), kind=kCustom, calls=%fused_computation.2.clone | custom fusion | bytes 8388736 | tf_op jit(solution)/shard_map/jit(_take)/gather | solution.py:36
  12.4 5.0 %gather_fusion.1 = bf16[32,128,512]{2,1,0:T(8,128)(2,1)} fusion(bf16[32,128,512]{2,1,0:T(8,128)(2,1)} %bitcast.134, s32[1024]{0:T(1024)S(1)} %pad_clamp_fusion.2), kind=kCustom, calls=%fused_computation.1.clone | custom fusion | bytes 8388736 | tf_op jit(solution)/shard_map/jit(_take)/gather | solution.py:36
  17.4 4.9 %gather_fusion.3 = bf16[32,128,512]{2,1,0:T(8,128)(2,1)} fusion(bf16[32,128,512]{2,1,0:T(8,128)(2,1)} %bitcast.135, s32[1024]{0:T(1024)S(1)} %pad_clamp_fusion), kind=kCustom, calls=%fused_computation.3.clone | custom fusion | bytes 8388736 | tf_op jit(solution)/shard_map/jit(_take)/gather | solution.py:36
  22.3 5.0 %gather_fusion = bf16[32,128,512]{2,1,0:T(8,128)(2,1)} fusion(bf16[32,128,512]{2,1,0:T(8,128)(2,1)} %bitcast.136, s32[1024]{0:T(1024)S(1)} %pad_clamp_fusion.3), kind=kCustom, calls=%fused_computation.clone | custom fusion | bytes 8388736 | tf_op jit(solution)/shard_map/jit(_take)/gather | solution.py:36
  27.3 7.2 %fusion.2 = f32[32,128,512]{2,1,0:T(8,128)} fusion(bf16[32,128,512]{2,1,0:T(8,128)(2,1)} %gather_fusion.2, pred[32]{0:T(512)(128)(4,1)S(1)} %get-tuple-element.22, bf16[32,4,128,128]{3,2,1,0:T(8,128)(2,1)} %param.15, pred[32]{0:T(512)(128)(4,1)S(1)} %get-tuple-element.28), kind=kOutput, calls=%fused_computation.9 | convolution fusion | flops 539492352 | bytes 13631552 | tf_op jit(solution)/shard_map/bij,bjs->bis/dot_general | solution.py:37
  34.5 4.5 %fusion.4 = f32[32,128,512]{2,1,0:T(8,128)} fusion(bf16[32,128,512]{2,1,0:T(8,128)(2,1)S(1)} %copy-done.2, pred[32]{0:T(512)(128)(4,1)S(1)} %get-tuple-element.18, bf16[32,4,128,128]{3,2,1,0:T(8,128)(2,1)S(1)} %copy-done.4, pred[32]{0:T(512)(128)(4,1)S(1)} %get-tuple-element.30), kind=kOutput, calls=%fused_computation.11 | convolution fusion | flops 539492352 | bytes 13632512 | tf_op jit(solution)/shard_map/bij,bjs->bis/dot_general | solution.py:37
  39.0 4.5 %fusion = f32[32,128,512]{2,1,0:T(8,128)} fusion(bf16[32,128,512]{2,1,0:T(8,128)(2,1)S(1)} %copy-done.3, pred[32]{0:T(512)(128)(4,1)S(1)} %get-tuple-element.20, bf16[32,4,128,128]{3,2,1,0:T(8,128)(2,1)S(1)} %copy-done.4, pred[32]{0:T(512)(128)(4,1)S(1)} %get-tuple-element.29), kind=kOutput, calls=%fused_computation.7 | convolution fusion | flops 539492352 | bytes 13632512 | tf_op jit(solution)/shard_map/bij,bjs->bis/dot_general | solution.py:37
  43.5 11.6 %add_convert_fusion = bf16[32,128,512]{2,1,0:T(8,128)(2,1)S(1)} fusion(f32[32,128,512]{2,1,0:T(8,128)} %fusion, f32[32,128,512]{2,1,0:T(8,128)} %fusion.2, f32[32,128,512]{2,1,0:T(8,128)} %fusion.4, bf16[32,128,512]{2,1,0:T(8,128)(2,1)} %gather_fusion, pred[32]{0:T(512)(128)(4,1)S(1)} %get-tuple-element.6, bf16[32,4,128,128]{3,2,1,0:T(8,128)(2,1)} %param.15, ...), kind=kOutput, calls=%fused_computation.4 | convolution fusion | flops 547880960 | bytes 34603072 | tf_op jit(solution)/shard_map/bij,bjs->bis/dot_general | solution.py:37
  60.5 30.1 %reduce-scatter.2.cloned.1.call-done = f32[128,512]{1,0:T(8,128)} async-done(((f32[512,512]{1,0:T(8,128)}), f32[128,512]{1,0:T(8,128)}) %reduce-scatter.2.cloned.1.call-update) | async-done | bytes 262160 | tf_op jit(solution)/shard_map/reduce_scatter | solution.py:56
  93.5 32.4 %all-reduce.3.cloned.1.call-done = f32[128,128]{0,1:T(8,128)} async-done(((f32[128,128]{0,1:T(8,128)}), f32[128,128]{0,1:T(8,128)}) %all-reduce.3.cloned.1.call-update) | async-done | bytes 65552 | tf_op jit(solution)/shard_map/psum | solution.py:66
  127.7 11.7 %cholesky.84 = f32[128,128]{1,0:T(8,128)S(1)} custom-call(f32[128,128]{1,0:T(8,128)S(1)} %fusion.55), custom_call_target="Cholesky" | custom-call | tf_op jit(solution)/shard_map/jit(cholesky)/cholesky | solution.py:67
  140.7 9.8 %custom-call.14 = f32[1,128,128]{1,2,0:T(8,128)S(1)} custom-call(f32[1,128,128]{2,1,0:T(8,128)S(1)} %fusion.44), custom_call_target="InvertDiagBlocksLowerTriangular" | custom-call | tf_op jit(solution)/shard_map/triangular_solve/custom-call.2 | solution.py:68
  150.8 14.4 %all_gather.18 = f32[512,128]{0,1:T(8,128)S(1)} all-gather(f32[128,128]{0,1:T(8,128)S(1)} %convolution_bitcast_fusion.4), channel_id=1, replica_groups=mesh['groups'=2,'snap'=4,'space'=4] {'space'}, dimensions={0}, use_global_device_ids=true | all-gather | bytes 327680 | tf_op jit(solution)/shard_map/all_gather | solution.py:71
  167.7 33.4 %all-reduce.5.cloned.1.call-done = f32[128,128]{0,1:T(8,128)} async-done(((f32[128,128]{0,1:T(8,128)}), f32[128,128]{0,1:T(8,128)}) %all-reduce.5.cloned.1.call-update) | async-done | bytes 65552 | tf_op jit(solution)/shard_map/psum | solution.py:66
  202.9 11.7 %cholesky.95 = f32[128,128]{1,0:T(8,128)S(1)} custom-call(f32[128,128]{1,0:T(8,128)S(1)} %fusion.53), custom_call_target="Cholesky" | custom-call | tf_op jit(solution)/shard_map/jit(cholesky)/cholesky | solution.py:67
  216.0 9.8 %custom-call.15 = f32[1,128,128]{1,2,0:T(8,128)S(1)} custom-call(f32[1,128,128]{2,1,0:T(8,128)S(1)} %fusion.45), custom_call_target="InvertDiagBlocksLowerTriangular" | custom-call | tf_op jit(solution)/shard_map/triangular_solve/custom-call.2 | solution.py:68
  226.1 12.3 %all_gather.19 = bf16[512,128]{0,1:T(8,128)(2,1)S(1)} all-gather(bf16[128,128]{0,1:T(8,128)(2,1)S(1)} %convolution_bitcast_fusion.3), channel_id=1, replica_groups=mesh['groups'=2,'snap'=4,'space'=4] {'space'}, dimensions={0}, use_global_device_ids=true | all-gather | bytes 163840 | tf_op jit(solution)/shard_map/all_gather | solution.py:71
  246.8 26.4 %all-gather.5.cloned.1.call-done = f32[1024,256]{1,0:T(8,128)} async-done(((f32[256,256]{1,0:T(8,128)}), f32[1024,256]{1,0:T(8,128)}) %all-gather.5.cloned.1.call-update) | async-done | bytes 1048592 | tf_op jit(solution)/shard_map/all_gather | solution.py:92
  275.4 11.7 %custom-call.16 = f32[1,128,128]{2,1,0:T(8,128)S(1)} custom-call(f32[1,128,128]{2,1,0:T(8,128)S(1)} %fusion.49), custom_call_target="Cholesky" | custom-call | tf_op jit(solution)/shard_map/vmap(jit(cholesky))/cholesky | solution.py:21
  288.5 9.8 %custom-call.17 = f32[1,1,128,128]{2,3,1,0:T(8,128)S(1)} custom-call(f32[1,1,128,128]{3,2,1,0:T(8,128)S(1)} %fusion.46), custom_call_target="InvertDiagBlocksLowerTriangular" | custom-call | tf_op jit(solution)/shard_map/vmap()/triangular_solve/custom-call.3 | solution.py:22
  302.5 22.9 %collective-permute-done.1 = bf16[4096,128]{0,1:T(8,128)(2,1)S(1)} collective-permute-done((bf16[4096,128]{0,1:T(8,128)(2,1)S(1)}, bf16[4096,128]{0,1:T(8,128)(2,1)S(1)}, u32[]{:S(2)}, u32[]{:S(2)}) %collective-permute-start.1) | collective-permute-done | bytes 1048608 | tf_op jit(solution)/shard_map/ppermute | solution.py:16
  327.3 28.1 %all-gather.7.cloned.1.call-done = f32[1024,256]{1,0:T(8,128)} async-done(((f32[256,256]{1,0:T(8,128)}), f32[1024,256]{1,0:T(8,128)}) %all-gather.7.cloned.1.call-update) | async-done | bytes 1048592 | tf_op jit(solution)/shard_map/all_gather | solution.py:92
  357.6 11.9 %custom-call.18 = f32[1,128,128]{2,1,0:T(8,128)S(1)} custom-call(f32[1,128,128]{2,1,0:T(8,128)S(1)} %fusion.48), custom_call_target="Cholesky" | custom-call | tf_op jit(solution)/shard_map/vmap(jit(cholesky))/cholesky | solution.py:21
  370.9 9.8 %custom-call.19 = f32[1,1,128,128]{2,3,1,0:T(8,128)S(1)} custom-call(f32[1,1,128,128]{3,2,1,0:T(8,128)S(1)} %fusion.47), custom_call_target="InvertDiagBlocksLowerTriangular" | custom-call | tf_op jit(solution)/shard_map/vmap()/triangular_solve/custom-call.3 | solution.py:22
  (75 shorter events, 43.4 us)
Async XLA Ops:
  6.5 268.0 %copy-start = (f32[3,256,128]{2,1,0:T(8,128)S(1)}, f32[3,256,128]{2,1,0:T(8,128)}, u32[]{:S(2)}) copy-start(f32[3,256,128]{2,1,0:T(8,128)} %param.19) | copy-start | bytes 1179652
  6.5 84.1 %reduce-scatter.2.cloned.1.call-start = ((), (), s32[]{:S(2)}) async-start(), calls=%async_computation.1 | async-start | bytes 1310720 | tf_op jit(solution)/shard_map/reduce_scatter | solution.py:56
  27.3 7.2 %copy-start.2 = (bf16[32,128,512]{2,1,0:T(8,128)(2,1)S(1)}, bf16[32,128,512]{2,1,0:T(8,128)(2,1)}, u32[]{:S(2)}) copy-start(bf16[32,128,512]{2,1,0:T(8,128)(2,1)} %gather_fusion.1) | copy-start | bytes 12582916
  27.3 7.2 %copy-start.4 = (bf16[32,4,128,128]{3,2,1,0:T(8,128)(2,1)S(1)}, bf16[32,4,128,128]{3,2,1,0:T(8,128)(2,1)}, u32[]{:S(2)}) copy-start(bf16[32,4,128,128]{3,2,1,0:T(8,128)(2,1)} %param.15) | copy-start | bytes 12582916
  34.5 4.5 %copy-start.3 = (bf16[32,128,512]{2,1,0:T(8,128)(2,1)S(1)}, bf16[32,128,512]{2,1,0:T(8,128)(2,1)}, u32[]{:S(2)}) copy-start(bf16[32,128,512]{2,1,0:T(8,128)(2,1)} %gather_fusion.3) | copy-start | bytes 12582916
  55.2 1.9 copy-start.1
  57.1 33.5 %copy-start.5 = (f32[512,128]{1,0:T(8,128)S(1)}, f32[512,128]{1,0:T(8,128)}, u32[]{:S(2)}) copy-start(f32[512,128]{1,0:T(8,128)} %param.18) | copy-start | bytes 786436
  60.4 65.4 %all-reduce.3.cloned.1.call-start = ((), (), s32[]{:S(2)}) async-start(), calls=%async_computation.2 | async-start | bytes 131072 | tf_op jit(solution)/shard_map/psum | solution.py:66
  92.9 108.2 %all-reduce.5.cloned.1.call-start = ((), (), s32[]{:S(2)}) async-start(), calls=%async_computation.3 | async-start | bytes 131072 | tf_op jit(solution)/shard_map/psum | solution.py:66
  167.5 105.7 %all-gather.5.cloned.1.call-start = ((), (), s32[]{:S(2)}) async-start(), calls=%async_computation.4 | async-start | bytes 1310720 | tf_op jit(solution)/shard_map/all_gather | solution.py:92
  242.0 2.7 collective-permute-start
  244.7 1.8 copy-start.7
  246.6 108.8 %all-gather.7.cloned.1.call-start = ((), (), s32[]{:S(2)}) async-start(), calls=%async_computation.5 | async-start | bytes 1310720 | tf_op jit(solution)/shard_map/all_gather | solution.py:92
  301.0 24.5 %collective-permute-start.1 = (bf16[4096,128]{0,1:T(8,128)(2,1)S(1)}, bf16[4096,128]{0,1:T(8,128)(2,1)S(1)}, u32[]{:S(2)}, u32[]{:S(2)}) collective-permute-start(bf16[4096,128]{0,1:T(8,128)(2,1)S(1)} %convolution_convert_fusion), channel_id=1, source_target_pairs={{0,8},{8,0},{4,12},{12,4},{1,9},{9,1},{5,13},{13,5},{2,10},{10,2},... | collective-permute-start | bytes 3145736 | tf_op jit(solution)/shard_map/ppermute | solution.py:16
  325.5 1.8 copy-start.6
Sparse Core Ops, SparseCore 0:
  60.6 29.9 reduce-scatter.1
  93.0 32.8 all-reduce.2
  167.6 33.4 all-reduce.4
  246.7 26.4 all-gather.4
  327.5 27.9 all-gather.6
